TPU v7x, 256 devices: a whole 4x4x8 slice. The times are simulated.
256 devices in a mesh: orb: 8 (over x, core), dom: 32 (over y, z).
Axes of the slice: x: 4, y: 4, z: 8, core: 2. Of those that a mesh axis runs over, the one named last changes fastest.
Arguments:
- orbitals: float32 [768, 128, 8, 128], P('orb', 'dom'), may hold values from -6 to 6
- potential: float32 [128, 8, 128], P('dom'), may hold values from -1 to 3
- prev_gradient: float32 [768, 128, 8, 128], P('orb', 'dom'), may hold values from -24 to 24
- prev_direction: float32 [768, 128, 8, 128], P('orb', 'dom'), may hold values from -24 to 24
Outputs:
- new_orbitals: float32 [768, 128, 8, 128], P('orb', 'dom')
- new_direction: float32 [768, 128, 8, 128], P('orb', 'dom')
- gradient: float32 [768, 128, 8, 128], P('orb', 'dom')
All inputs are finite; a program needn't handle non-finite values.
Results may differ from a plain program's by a relative error of at most 0.0002.
Values sent between devices are 32-bit elements; how exact they have to be, the bound alone decides.
No kernel may reach another device: no remote copies, remote signals or barrier semaphores. Data moves between devices by JAX's collectives and lax.ppermute only.
A program may use at most 128 MiB of HBM per device.

v0:
```python
import jax
import jax.numpy as jnp
from jax import lax
from jax.sharding import PartitionSpec as P

coeffs = (-205.0 / 72.0, 8.0 / 5.0, -1.0 / 5.0, 8.0 / 315.0, -1.0 / 560.0)
step_length = 0.05


def padded_2(cells, sides, width):
    for axis, dim in sides:
        count = lax.axis_size(axis)
        ends = count - 1
        head = lax.slice_in_dim(cells, 0, width, axis=dim)
        tail = lax.slice_in_dim(cells, cells.shape[dim] - width, cells.shape[dim], axis=dim)
        cells = jnp.concatenate(
            [
                lax.ppermute(tail, axis, [(i, (i + 1) % count) for i in range(ends)]),
                cells,
                lax.ppermute(head, axis, [((i + 1) % count, i) for i in range(ends)]),
            ],
            axis=dim,
        )
    return cells


def laplace(padded, planes, lines, columns):
    center = padded[:, 4 : 4 + planes, 4 : 4 + lines, 4 : 4 + columns]
    total = 3.0 * coeffs[0] * center
    for offset in range(1, 5):
        total = total + coeffs[offset] * (
            padded[:, 4 + offset : 4 + offset + planes, 4 : 4 + lines, 4 : 4 + columns]
            + padded[:, 4 - offset : 4 - offset + planes, 4 : 4 + lines, 4 : 4 + columns]
        )
        total = total + coeffs[offset] * (
            padded[:, 4 : 4 + planes, 4 + offset : 4 + offset + lines, 4 : 4 + columns]
            + padded[:, 4 : 4 + planes, 4 - offset : 4 - offset + lines, 4 : 4 + columns]
        )
        total = total + coeffs[offset] * (
            padded[:, 4 : 4 + planes, 4 : 4 + lines, 4 + offset : 4 + offset + columns]
            + padded[:, 4 : 4 + planes, 4 : 4 + lines, 4 - offset : 4 - offset + columns]
        )
    return total


def highdot(left, right):
    return jnp.dot(left, right, precision=lax.Precision.HIGHEST, preferred_element_type=jnp.float32)


def on_device(orbitals, potential, prev_gradient, prev_direction):
    block = orbitals.shape[0]
    extended = padded_2(orbitals, (("dom", 1),), 4)
    padded = jnp.pad(extended, ((0, 0), (0, 0), (4, 4), (4, 4)))
    lap = laplace(padded, orbitals.shape[1], orbitals.shape[2], orbitals.shape[3])
    image = -0.5 * lap + potential[None] * orbitals
    cmat = orbitals.reshape(block, -1)
    hmat_rows = image.reshape(block, -1)
    cells = cmat.shape[1] * lax.axis_size("dom")
    cell_orbs, cell_images = (
        lax.all_to_all(cmat, "orb", split_axis=1, concat_axis=0, tiled=True),
        lax.all_to_all(hmat_rows, "orb", split_axis=1, concat_axis=0, tiled=True),
    )
    correlation, hamilton = lax.psum(
        (highdot(cell_orbs, cell_orbs.T), highdot(cell_orbs, cell_images.T)), ("orb", "dom")
    )
    correlation = correlation / cells
    hamilton = hamilton / cells
    cell_grad = (
        4.0 * cell_images
        - 2.0 * highdot(correlation.T, cell_images)
        - 2.0 * highdot(hamilton.T, cell_orbs)
    )
    grad = lax.all_to_all(cell_grad, "orb", split_axis=0, concat_axis=1, tiled=True)
    grad = grad.reshape(orbitals.shape)
    both, cross, before = lax.psum(
        (
            jnp.sum(grad * grad),
            jnp.sum(grad * prev_gradient),
            jnp.sum(prev_gradient * prev_gradient),
        ),
        ("orb", "dom"),
    )
    beta = (both - cross) / before
    direction = -grad + beta * prev_direction
    return (orbitals + step_length * direction, direction, grad)


def solution(mesh):
    in_specs = (
        P("orb", "dom", None, None),
        P("dom", None, None),
        P("orb", "dom", None, None),
        P("orb", "dom", None, None),
    )
    out_specs = (
        P("orb", "dom", None, None),
        P("orb", "dom", None, None),
        P("orb", "dom", None, None),
    )
    return jax.shard_map(
        on_device, mesh=mesh, in_specs=in_specs, out_specs=out_specs, check_vma=False
    )
```

profile of v0, /device:TPU:1, one launch (start us, length us, event | category | flops | bytes accessed | tf_op | source)
XLA Modules:
  0.0 553.9 jit_solution(16415115841045701364)
XLA Ops:
  7.2 5.5 collective-permute-start.1
  12.7 1.3 collective-permute-start
  14.0 1.5 all_to_all.44
  15.5 2.1 copy.16
  17.6 5.3 all-to-all-start.1
  22.8 22.1 %collective-permute-done.1 = f32[96,4,8,128]{3,2,1,0:T(8,128)} collective-permute-done((f32[96,4,8,128]{3,2,1,0:T(8,128)}, f32[96,4,8,128]{3,2,1,0:T(8,128)}, u32[]{:S(2)}, u32[]{:S(2)}) %collective-permute-start.1) | collective-permute-done | bytes 1572896 | tf_op jit(solution)/shard_map/ppermute | solution.py:18
  44.9 2.7 constant_dynamic-update-slice_fusion.3
  47.6 0.0 copy-done
  47.6 2.1 constant_dynamic-update-slice_fusion.1
  49.8 0.1 collective-permute-done
  49.9 11.4 %select_maximum_fusion = f32[96,12,16,136]{3,2,1,0:T(8,128)} fusion(f32[96,4,8,128]{3,2,1,0:T(8,128)} %collective-permute-done, f32[96,4,8,128]{3,2,1,0:T(8,128)S(1)} %copy-done, f32[96,4,8,128]{3,2,1,0:T(8,128)} %collective-permute-done.1), kind=kLoop, calls=%fused_computation.4 | loop fusion | flops 37601280 | bytes 14745600 | tf_op jit(solution)/shard_map/concatenate | solution.py:16
  61.3 2.8 constant_dynamic-update-slice_fusion
  64.0 41.4 %fusion.10 = f32[96,4,8,128]{3,2,1,0:T(8,128)} fusion(f32[96,12,16,136]{3,2,1,0:T(8,128)} %select_maximum_fusion, f32[96,8,8,128]{3,2,1,0:T(8,128)} %get-tuple-element.13, f32[96,8,8,128]{3,2,1,0:T(8,128)} %constant_dynamic-update-slice_fusion, f32[96,4,8,128]{3,2,1,0:T(8,128)S(1)} %copy-done, f32[96,4,8,128]{3,2,1,0:T(8,128)} %collective-permute-done, ...), kind=kLoop, calls=%fused_computation.18 | loop fusion | flops 15728640 | bytes 40910848 | tf_op jit(solution)/shard_map/add | solution.py:55
  105.5 2.6 all_to_all.40
  108.0 3.5 copy.15
  111.5 0.0 all-to-all-done.1
  111.5 6.1 %all-to-all-start = ((f32[96,8,512]{2,0,1:T(8,128)}), f32[96,8,512]{2,0,1:T(8,128)}, u32[]{:S(2)}, u32[]{:S(2)}) async-start(f32[96,8,512]{2,0,1:T(8,128)} %copy.15), calls=%async_computation | async-start | bytes 3145728 | tf_op jit(solution)/shard_map/all_to_all | solution.py:61
  117.6 0.0 all-reduce.5.cloned.1.call-start
  117.6 5.4 fusion.38
  123.0 15.3 %all-to-all-done = f32[96,8,512]{2,0,1:T(8,128)} async-done(((f32[96,8,512]{2,0,1:T(8,128)}), f32[96,8,512]{2,0,1:T(8,128)}, u32[]{:S(2)}, u32[]{:S(2)}) %all-to-all-start) | async-done | bytes 1572896 | tf_op jit(solution)/shard_map/all_to_all | solution.py:61
  138.3 6.8 %convolution_bitcast_fusion = f32[768,768]{1,0:T(8,128)} fusion(f32[768,512]{1,0:T(8,128)} %bitcast.1, f32[768,512]{1,0:T(8,128)S(1)} %bitcast.22), kind=kOutput, calls=%fused_computation.13 | convolution fusion | flops 3623878656 | bytes 5505024 | tf_op jit(solution)/shard_map/dot_general | solution.py:47
  145.1 0.0 all-reduce.5.cloned.1.call-update
  145.1 273.7 %all-reduce.5.cloned.1.call-done = (f32[768,768]{1,0:T(8,128)}, f32[768,768]{1,0:T(8,128)}) async-done(((f32[768,768]{1,0:T(8,128)}, f32[768,768]{1,0:T(8,128)}), (f32[768,768]{1,0:T(8,128)}, f32[768,768]{1,0:T(8,128)})) %all-reduce.5.cloned.1.call-update) | async-done | bytes 4718608 | tf_op jit(solution)/shard_map/psum | solution.py:63
  418.9 5.7 %fusion.3 = f32[768,512]{1,0:T(8,128)S(1)} fusion(f32[768,512]{1,0:T(8,128)S(1)} %bitcast.23, f32[768,768]{1,0:T(8,128)} %get-tuple-element.8), kind=kOutput, calls=%fused_computation.9 | convolution fusion | flops 3624468480 | bytes 5505024 | tf_op jit(solution)/shard_map/dot_general | solution.py:47
  424.6 6.3 %multiply_subtract_fusion = f32[768,512]{1,0:T(8,128)S(1)} fusion(f32[768,512]{1,0:T(8,128)S(1)} %fusion.3, f32[768,512]{1,0:T(8,128)} %bitcast.1, f32[768,768]{1,0:T(8,128)S(1)} %copy-done.1), kind=kOutput, calls=%fused_computation.55 | convolution fusion | flops 3626434560 | bytes 7077888 | tf_op jit(solution)/shard_map/dot_general | solution.py:47
  430.9 27.0 %all_to_all.54 = f32[8,96,512]{2,1,0:T(8,128)S(1)} all-to-all(f32[8,96,512]{2,1,0:T(8,128)S(1)} %bitcast.25), channel_id=1, replica_groups=mesh['orb'=8,'dom'=32] {'orb'}, dimensions={0} | all-to-all | bytes 3145728 | tf_op jit(solution)/shard_map/all_to_all | solution.py:73
  457.9 2.1 copy.18
  459.9 2.4 reshape.24
  462.4 2.9 multiply_reduce_fusion
  465.3 1.0 multiply_reduce_fusion.2
  466.3 74.7 %all-reduce.1 = (f32[]{:T(128)}, f32[]{:T(128)}, f32[]{:T(128)}) all-reduce(f32[]{:T(128)} %multiply_reduce_fusion.2, f32[]{:T(128)} %get-tuple-element.4, f32[]{:T(128)} %get-tuple-element.3), channel_id=1, replica_groups=mesh['orb'=8,'dom'=32] {'orb','dom'}, use_global_device_ids=true, to_apply=%region_3.4 | all-reduce | flops 3 | bytes 24 | tf_op jit(solution)/shard_map/psum | solution.py:75
  542.9 4.1 multiply_add_fusion
  (5 shorter events, 0.0 us)
Async XLA Ops:
  7.2 37.7 %collective-permute-start.1 = (f32[96,4,8,128]{3,2,1,0:T(8,128)}, f32[96,4,8,128]{3,2,1,0:T(8,128)}, u32[]{:S(2)}, u32[]{:S(2)}) collective-permute-start(f32[96,4,8,128]{3,2,1,0:T(8,128)} %param.4), channel_id=1, source_target_pairs={{0,1},{1,2},{2,3},{3,4},{4,5},{5,6},{6,7},{7,8},{8,9},{9,10},{10,1... | collective-permute-start | bytes 4718600 | tf_op jit(solution)/shard_map/ppermute | solution.py:18
  12.7 37.2 %collective-permute-start = (f32[96,4,8,128]{3,2,1,0:T(8,128)}, f32[96,4,8,128]{3,2,1,0:T(8,128)}, u32[]{:S(2)}, u32[]{:S(2)}) collective-permute-start(f32[96,4,8,128]{3,2,1,0:T(8,128)} %param.4), channel_id=1, source_target_pairs={{1,0},{2,1},{3,2},{4,3},{5,4},{6,5},{7,6},{8,7},{9,8},{10,9},{11,1... | collective-permute-start | bytes 4718600 | tf_op jit(solution)/shard_map/ppermute | solution.py:20
  17.6 93.9 %all-to-all-start.1 = ((f32[96,8,512]{2,0,1:T(8,128)}), f32[96,8,512]{2,0,1:T(8,128)S(1)}, u32[]{:S(2)}, u32[]{:S(2)}) async-start(f32[96,8,512]{2,0,1:T(8,128)} %copy.16), calls=%async_computation.1 | async-start | bytes 3145728 | tf_op jit(solution)/shard_map/all_to_all | solution.py:60
  22.8 24.8 %copy-start = (f32[96,4,8,128]{3,2,1,0:T(8,128)S(1)}, f32[96,4,8,128]{3,2,1,0:T(8,128)}, u32[]{:S(2)}) copy-start(f32[96,4,8,128]{3,2,1,0:T(8,128)} %param.4) | copy-start | bytes 4718596
  61.3 2.8 copy-start.2
  111.5 26.8 %all-to-all-start = ((f32[96,8,512]{2,0,1:T(8,128)}), f32[96,8,512]{2,0,1:T(8,128)}, u32[]{:S(2)}, u32[]{:S(2)}) async-start(f32[96,8,512]{2,0,1:T(8,128)} %copy.15), calls=%async_computation | async-start | bytes 3145728 | tf_op jit(solution)/shard_map/all_to_all | solution.py:61
  117.6 301.2 %all-reduce.5.cloned.1.call-start = ((), (), s32[]{:S(2)}) async-start(), calls=%async_computation.3 | async-start | bytes 9437184 | tf_op jit(solution)/shard_map/psum | solution.py:63
  418.9 5.7 %copy-start.1 = (f32[768,768]{1,0:T(8,128)S(1)}, f32[768,768]{1,0:T(8,128)}, u32[]{:S(2)}) copy-start(f32[768,768]{1,0:T(8,128)} %get-tuple-element.9) | copy-start | bytes 7077892
Sparse Core Ops, SparseCore 0:
  145.2 273.5 all-reduce.4
where the time goes:
time: 555 us; the launch traced here: 554 us
  waiting for transfers between devices  311 us (56%)
  blocking collectives  102 us (18%)
  other arithmetic  60.9 us (11%)
  matrix products  24.2 us (4%)
  local copies, waits for them, and re-layouts  21.7 us (4%)
  starting transfers between devices  18.2 us (3%)
  between operations  16 us (3%)
    psum x1, waiting for transfers between devices, on_device(): lax.psum((highdot(cell_orbs, cell_orbs.T), highdot(cell_orbs, cell_images...  274 us
    psum x1, blocking collectives, on_device(): lax.psum((jnp.sum(grad * grad), jnp.sum(grad * prev_gradient), jnp.sum(pr...  74.7 us
    add x1, other arithmetic, on_device(): image = -0.5 * lap + potential[None] * orbitals  41.4 us
    all_to_all x1, blocking collectives, on_device(): lax.all_to_all(cell_grad, 'orb', split_axis=0, concat_axis=1, tiled=True)  27 us
    dot_general x4, matrix products, highdot(): jnp.dot(left, right, precision=lax.Precision.HIGHEST, preferred_element_t...  24.2 us
    ppermute x1, waiting for transfers between devices, padded_2(): lax.ppermute(tail, axis, [(i, (i + 1) % count) for i in range(ends)])  22.1 us
    all_to_all x1, waiting for transfers between devices, on_device(): lax.all_to_all(hmat_rows, 'orb', split_axis=1, concat_axis=0, tiled=True)  15.3 us
    concatenate x1, other arithmetic, padded_2(): jnp.concatenate([lax.ppermute(tail, axis, [(i, (i + 1) % count) for i in...  11.4 us
  transfers between devices with their start and end apart: 5, of which 4 were waited for; matrix products, arithmetic and copies ran while one was open for 13% of the time, Pallas kernels for 0%

commit v1 on v0

--- a/solution.py
+++ b/solution.py
@@ -61,7 +61,7 @@
         lax.all_to_all(hmat_rows, "orb", split_axis=1, concat_axis=0, tiled=True),
     )
     correlation, hamilton = lax.psum(
-        (highdot(cell_orbs, cell_orbs.T), highdot(cell_orbs, cell_images.T)), ("orb", "dom")
+        lax.psum((highdot(cell_orbs, cell_orbs.T), highdot(cell_orbs, cell_images.T)), "orb"), "dom"
     )
     correlation = correlation / cells
     hamilton = hamilton / cells

time: 555 us -> 532 us (0.959)
  waiting for transfers between devices: 311 us -> 290 us
    psum x1, waiting for transfers between devices: 274 us -> 80.6 us  [on_device(): lax.psum((highdot(cell_orbs, cell_orbs.T), highdot(cell_orbs, cell_images...]
    psum x0 -> x1, waiting for transfers between devices: none -> 172 us  [on_device(): lax.psum(lax.psum((highdot(cell_orbs, cell_orbs.T), highdot(cell_orbs, ce...]
  transfers between devices with their start and end apart: 5 -> 6, of which waited for: 4 -> 5; matrix products, arithmetic and copies ran while one was open for 13% -> 13% of each run, Pallas kernels for 0% -> 0%
where the time goes in v1:
time: 532 us
  waiting for transfers between devices  290 us (55%)
  blocking collectives  100 us (19%)
  other arithmetic  60.7 us (11%)
  matrix products  24 us (5%)
  local copies, waits for them, and re-layouts  21.7 us (4%)
  starting transfers between devices  18.4 us (3%)
  between operations  16.1 us (3%)
    psum x1, waiting for transfers between devices, on_device(): lax.psum(lax.psum((highdot(cell_orbs, cell_orbs.T), highdot(cell_orbs, ce...  172 us
    psum x1, waiting for transfers between devices, on_device(): lax.psum((highdot(cell_orbs, cell_orbs.T), highdot(cell_orbs, cell_images...  80.6 us
    psum x1, blocking collectives, on_device(): lax.psum((jnp.sum(grad * grad), jnp.sum(grad * prev_gradient), jnp.sum(pr...  74.2 us
    add x1, other arithmetic, on_device(): image = -0.5 * lap + potential[None] * orbitals  41.3 us
    all_to_all x1, blocking collectives, on_device(): lax.all_to_all(cell_grad, 'orb', split_axis=0, concat_axis=1, tiled=True)  26.2 us
    dot_general x4, matrix products, highdot(): jnp.dot(left, right, precision=lax.Precision.HIGHEST, preferred_element_t...  24 us
    ppermute x1, waiting for transfers between devices, padded_2(): lax.ppermute(tail, axis, [(i, (i + 1) % count) for i in range(ends)])  22.1 us
    all_to_all x1, waiting for transfers between devices, on_device(): lax.all_to_all(hmat_rows, 'orb', split_axis=1, concat_axis=0, tiled=True)  15.3 us
  transfers between devices with their start and end apart: 6, of which 5 were waited for; matrix products, arithmetic and copies ran while one was open for 13% of the time, Pallas kernels for 0%

profile of v1, /device:TPU:1, one launch (start us, length us, event | category | flops | bytes accessed | tf_op | source)
XLA Modules:
  0.0 531.6 jit_solution(4288899238009871594)
XLA Ops:
  7.2 5.5 %collective-permute-start.1 = (f32[96,4,8,128]{3,2,1,0:T(8,128)}, f32[96,4,8,128]{3,2,1,0:T(8,128)}, u32[]{:S(2)}, u32[]{:S(2)}) collective-permute-start(f32[96,4,8,128]{3,2,1,0:T(8,128)} %param.4), channel_id=1, source_target_pairs={{0,1},{1,2},{2,3},{3,4},{4,5},{5,6},{6,7},{7,8},{8,9},{9,10},{10,1... | collective-permute-start | bytes 4718600 | tf_op jit(solution)/shard_map/ppermute | solution.py:18
  12.7 1.3 collective-permute-start
  14.0 1.5 all_to_all.44
  15.5 2.1 copy.16
  17.5 5.3 all-to-all-start.1
  22.8 22.1 %collective-permute-done.1 = f32[96,4,8,128]{3,2,1,0:T(8,128)} collective-permute-done((f32[96,4,8,128]{3,2,1,0:T(8,128)}, f32[96,4,8,128]{3,2,1,0:T(8,128)}, u32[]{:S(2)}, u32[]{:S(2)}) %collective-permute-start.1) | collective-permute-done | bytes 1572896 | tf_op jit(solution)/shard_map/ppermute | solution.py:18
  44.9 2.7 constant_dynamic-update-slice_fusion.3
  47.6 2.1 constant_dynamic-update-slice_fusion.1
  49.8 0.1 collective-permute-done
  49.9 11.4 %select_maximum_fusion = f32[96,12,16,136]{3,2,1,0:T(8,128)} fusion(f32[96,4,8,128]{3,2,1,0:T(8,128)} %collective-permute-done, f32[96,4,8,128]{3,2,1,0:T(8,128)S(1)} %copy-done, f32[96,4,8,128]{3,2,1,0:T(8,128)} %collective-permute-done.1), kind=kLoop, calls=%fused_computation.4 | loop fusion | flops 37601280 | bytes 14745600 | tf_op jit(solution)/shard_map/concatenate | solution.py:16
  61.3 2.7 constant_dynamic-update-slice_fusion
  64.0 41.3 %fusion.10 = f32[96,4,8,128]{3,2,1,0:T(8,128)} fusion(f32[96,12,16,136]{3,2,1,0:T(8,128)} %select_maximum_fusion, f32[96,8,8,128]{3,2,1,0:T(8,128)} %get-tuple-element.15, f32[96,8,8,128]{3,2,1,0:T(8,128)} %constant_dynamic-update-slice_fusion, f32[96,4,8,128]{3,2,1,0:T(8,128)S(1)} %copy-done, f32[96,4,8,128]{3,2,1,0:T(8,128)} %collective-permute-done, ...), kind=kLoop, calls=%fused_computation.18 | loop fusion | flops 15728640 | bytes 40910848 | tf_op jit(solution)/shard_map/add | solution.py:55
  105.3 2.6 all_to_all.40
  107.9 3.5 copy.15
  111.3 6.1 %all-to-all-start = ((f32[96,8,512]{2,0,1:T(8,128)}), f32[96,8,512]{2,0,1:T(8,128)}, u32[]{:S(2)}, u32[]{:S(2)}) async-start(f32[96,8,512]{2,0,1:T(8,128)} %copy.15), calls=%async_computation | async-start | bytes 3145728 | tf_op jit(solution)/shard_map/all_to_all | solution.py:61
  117.5 5.4 %fusion.38 = f32[768,768]{1,0:T(8,128)} fusion(f32[768,512]{1,0:T(8,128)S(1)} %bitcast.21), kind=kOutput, calls=%fused_computation.64 | convolution fusion | flops 3623878656 | bytes 3932160 | tf_op jit(solution)/shard_map/dot_general | solution.py:47
  122.9 15.3 %all-to-all-done = f32[96,8,512]{2,0,1:T(8,128)} async-done(((f32[96,8,512]{2,0,1:T(8,128)}), f32[96,8,512]{2,0,1:T(8,128)}, u32[]{:S(2)}, u32[]{:S(2)}) %all-to-all-start) | async-done | bytes 1572896 | tf_op jit(solution)/shard_map/all_to_all | solution.py:61
  138.1 6.8 %convolution_bitcast_fusion = f32[768,768]{1,0:T(8,128)} fusion(f32[768,512]{1,0:T(8,128)} %bitcast.1, f32[768,512]{1,0:T(8,128)S(1)} %bitcast.22), kind=kOutput, calls=%fused_computation.13 | convolution fusion | flops 3623878656 | bytes 5505024 | tf_op jit(solution)/shard_map/dot_general | solution.py:47
  144.9 0.0 all-reduce.9.cloned.1.call-update
  145.0 0.3 all-reduce.7.cloned.1.call-start
  145.2 80.6 %all-reduce.9.cloned.1.call-done = (f32[768,768]{1,0:T(8,128)}, f32[768,768]{1,0:T(8,128)}) async-done(((f32[768,768]{1,0:T(8,128)}, f32[768,768]{1,0:T(8,128)}), (f32[768,768]{1,0:T(8,128)}, f32[768,768]{1,0:T(8,128)})) %all-reduce.9.cloned.1.call-update) | async-done | bytes 4718608 | tf_op jit(solution)/shard_map/psum | solution.py:64
  225.8 0.0 all-reduce.7.cloned.1.call-update
  225.8 172.2 %all-reduce.7.cloned.1.call-done = (f32[768,768]{1,0:T(8,128)}, f32[768,768]{1,0:T(8,128)}) async-done(((f32[768,768]{1,0:T(8,128)}, f32[768,768]{1,0:T(8,128)}), (f32[768,768]{1,0:T(8,128)}, f32[768,768]{1,0:T(8,128)})) %all-reduce.7.cloned.1.call-update) | async-done | bytes 4718608 | tf_op jit(solution)/shard_map/psum | solution.py:63
  398.0 5.7 %fusion.3 = f32[768,512]{1,0:T(8,128)S(1)} fusion(f32[768,512]{1,0:T(8,128)S(1)} %bitcast.23, f32[768,768]{1,0:T(8,128)} %get-tuple-element.8), kind=kOutput, calls=%fused_computation.9 | convolution fusion | flops 3624468480 | bytes 5505024 | tf_op jit(solution)/shard_map/dot_general | solution.py:47
  403.7 6.0 %multiply_subtract_fusion = f32[768,512]{1,0:T(8,128)S(1)} fusion(f32[768,512]{1,0:T(8,128)S(1)} %fusion.3, f32[768,512]{1,0:T(8,128)} %bitcast.1, f32[768,768]{1,0:T(8,128)S(1)} %copy-done.1), kind=kOutput, calls=%fused_computation.55 | convolution fusion | flops 3626434560 | bytes 7077888 | tf_op jit(solution)/shard_map/dot_general | solution.py:47
  409.8 26.2 %all_to_all.54 = f32[8,96,512]{2,1,0:T(8,128)S(1)} all-to-all(f32[8,96,512]{2,1,0:T(8,128)S(1)} %bitcast.25), channel_id=1, replica_groups=mesh['orb'=8,'dom'=32] {'orb'}, dimensions={0} | all-to-all | bytes 3145728 | tf_op jit(solution)/shard_map/all_to_all | solution.py:73
  436.0 2.1 copy.18
  438.1 2.4 reshape.24
  440.5 2.9 multiply_reduce_fusion
  443.4 1.0 multiply_reduce_fusion.2
  444.4 74.2 %all-reduce.1 = (f32[]{:T(128)}, f32[]{:T(128)}, f32[]{:T(128)}) all-reduce(f32[]{:T(128)} %multiply_reduce_fusion.2, f32[]{:T(128)} %get-tuple-element.4, f32[]{:T(128)} %get-tuple-element.3), channel_id=1, replica_groups=mesh['orb'=8,'dom'=32] {'orb','dom'}, use_global_device_ids=true, to_apply=%region_5.6 | all-reduce | flops 3 | bytes 24 | tf_op jit(solution)/shard_map/psum | solution.py:75
  520.6 4.1 multiply_add_fusion
  (8 shorter events, 0.0 us)
Async XLA Ops:
  7.2 37.7 %collective-permute-start.1 = (f32[96,4,8,128]{3,2,1,0:T(8,128)}, f32[96,4,8,128]{3,2,1,0:T(8,128)}, u32[]{:S(2)}, u32[]{:S(2)}) collective-permute-start(f32[96,4,8,128]{3,2,1,0:T(8,128)} %param.4), channel_id=1, source_target_pairs={{0,1},{1,2},{2,3},{3,4},{4,5},{5,6},{6,7},{7,8},{8,9},{9,10},{10,1... | collective-permute-start | bytes 4718600 | tf_op jit(solution)/shard_map/ppermute | solution.py:18
  12.7 37.2 %collective-permute-start = (f32[96,4,8,128]{3,2,1,0:T(8,128)}, f32[96,4,8,128]{3,2,1,0:T(8,128)}, u32[]{:S(2)}, u32[]{:S(2)}) collective-permute-start(f32[96,4,8,128]{3,2,1,0:T(8,128)} %param.4), channel_id=1, source_target_pairs={{1,0},{2,1},{3,2},{4,3},{5,4},{6,5},{7,6},{8,7},{9,8},{10,9},{11,1... | collective-permute-start | bytes 4718600 | tf_op jit(solution)/shard_map/ppermute | solution.py:20
  17.5 93.8 %all-to-all-start.1 = ((f32[96,8,512]{2,0,1:T(8,128)}), f32[96,8,512]{2,0,1:T(8,128)S(1)}, u32[]{:S(2)}, u32[]{:S(2)}) async-start(f32[96,8,512]{2,0,1:T(8,128)} %copy.16), calls=%async_computation.1 | async-start | bytes 3145728 | tf_op jit(solution)/shard_map/all_to_all | solution.py:60
  22.8 24.8 %copy-start = (f32[96,4,8,128]{3,2,1,0:T(8,128)S(1)}, f32[96,4,8,128]{3,2,1,0:T(8,128)}, u32[]{:S(2)}) copy-start(f32[96,4,8,128]{3,2,1,0:T(8,128)} %param.4) | copy-start | bytes 4718596
  61.3 2.8 copy-start.2
  111.3 26.8 %all-to-all-start = ((f32[96,8,512]{2,0,1:T(8,128)}), f32[96,8,512]{2,0,1:T(8,128)}, u32[]{:S(2)}, u32[]{:S(2)}) async-start(f32[96,8,512]{2,0,1:T(8,128)} %copy.15), calls=%async_computation | async-start | bytes 3145728 | tf_op jit(solution)/shard_map/all_to_all | solution.py:61
  117.5 108.3 %all-reduce.9.cloned.1.call-start = ((), (), s32[]{:S(2)}) async-start(), calls=%async_computation.4 | async-start | bytes 9437184 | tf_op jit(solution)/shard_map/psum | solution.py:64
  145.0 253.0 %all-reduce.7.cloned.1.call-start = ((), (), s32[]{:S(2)}) async-start(), calls=%async_computation.3 | async-start | bytes 9437184 | tf_op jit(solution)/shard_map/psum | solution.py:63
  398.0 5.7 %copy-start.1 = (f32[768,768]{1,0:T(8,128)S(1)}, f32[768,768]{1,0:T(8,128)}, u32[]{:S(2)}) copy-start(f32[768,768]{1,0:T(8,128)} %get-tuple-element.9) | copy-start | bytes 7077892
Sparse Core Ops, SparseCore 0:
  145.1 80.6 all-reduce.8
  229.4 168.5 all-reduce.6
